TPU v7x, 256 devices: a whole 4x4x8 slice. The times are simulated.
256 devices in a mesh: grp: 16 (over x, y), seq: 16 (over z, core).
Axes of the slice: x: 4, y: 4, z: 8, core: 2. Of those that a mesh axis runs over, the one named last changes fastest.
Arguments:
- events: bfloat16 [65536, 1024], P(('grp', 'seq')), may hold values from -6 to 6
- lengths: int32 [256, 16], P(('grp', 'seq')), may hold values from 1 to 24, as said below
- destinations: int32 [256, 16], P(('grp', 'seq')), may hold values from 0 to 15, as said below
- history: int32 [65536], P(('grp', 'seq')), may hold values from 0 to 8191, as said below
- negatives: int32 [65536, 3], P(('grp', 'seq')), may hold values from 0 to 8191, as said below
- in_weight: bfloat16 [1024, 2048], replicated, may hold values from -0.1875 to 0.1875
- out_weight: bfloat16 [1024, 512], replicated, may hold values from -0.25 to 0.25
- item_table: bfloat16 [8192, 1024], P('seq'), may hold values from -0.1875 to 0.1875
Outputs:
- layer_out: bfloat16 [65536, 1024], P(('grp', 'seq'))
- in_grad: float32 [1024, 2048], P('seq')
- out_grad: float32 [1024, 512], P('seq')
- table_grad: float32 [8192, 1024], P('seq')
Inputs may be any that keep to these rules, and one draw needn't show every extreme that they name: Each loader device holds 16 users whose lengths sum to 256; the longest history is 24. `destinations`: the 16 users of a loader device go to the 16 different devices of its group, one to each, and every device of a group receives users with 256 rows in all. `history`: item i lies in row i % 512 of owner i // 512. The 4 candidates of an event lie on 4 different owners, and after the relayout every device holds exactly 64 candidates of each owner. `negatives`: numbered as history; see there.
All inputs are finite; a program needn't handle non-finite values.
Results may differ from a plain program's by a relative error of at most 0.02.
Values may be sent and summed in bfloat16 or wider, within the bound.
A program may use at most 128 MiB of HBM per device.

v0:
```python
import jax
import jax.numpy as jnp
from jax import lax
from jax.sharding import PartitionSpec as P

D = 1024
HEADS = 4
HEAD_DIM = 128
NCAND = 4
VOCAB_DEV = 512
epsilon = 1e-05
softmax_warmth = 0.05


def center_scale(values):
    average = jnp.mean(values, -1, keepdims=True)
    centered = values - average
    inverse = lax.rsqrt(jnp.mean(centered * centered, -1, keepdims=True) + epsilon)
    return (centered * inverse, inverse)


def silu_slope(values):
    sigmoid = jax.nn.sigmoid(values)
    return sigmoid * (1.0 + values * (1.0 - sigmoid))


def batch_stacked(pattern, first_operand, second_operand):
    return jnp.einsum(pattern, first_operand, second_operand, preferred_element_type=jnp.float32)


def layer_forward(tokens, attend_mask, in_weight, out_weight, batch_count):
    hidden_width = out_weight.shape[1]
    scoring_scale = HEAD_DIM ** (-0.5)
    features = tokens.astype(jnp.float32)
    normed_in = center_scale(features)[0].astype(jnp.bfloat16)
    preact = jnp.dot(normed_in, in_weight, preferred_element_type=jnp.float32)
    projected = jax.nn.silu(preact).astype(jnp.bfloat16)
    gate_part = projected[:, :hidden_width]
    value_portion = projected[:, hidden_width : 2 * hidden_width].reshape(
        batch_count, -1, hidden_width
    )
    query_portion = projected[:, 2 * hidden_width : 3 * hidden_width].reshape(
        batch_count, -1, hidden_width
    )
    key_portion = projected[:, 3 * hidden_width :].reshape(batch_count, -1, hidden_width)
    score_list, weight_pieces, output_pieces = ([], [], [])
    for current_head in range(HEADS):
        column_begin = current_head * HEAD_DIM
        column_end = column_begin + HEAD_DIM
        attention_scores = (
            batch_stacked(
                "ptx,pux->ptu",
                query_portion[..., column_begin:column_end],
                key_portion[..., column_begin:column_end],
            )
            * scoring_scale
        )
        attention_weight = (jax.nn.silu(attention_scores) * attend_mask).astype(jnp.bfloat16)
        output_pieces.append(
            batch_stacked(
                "fjz,fzy->fjy", attention_weight, value_portion[..., column_begin:column_end]
            )
        )
        score_list.append(attention_scores)
        weight_pieces.append(attention_weight)
    attended = jnp.concatenate(output_pieces, -1).reshape(-1, hidden_width)
    normed, inverse = center_scale(attended)
    gated_rows = (normed * gate_part.astype(jnp.float32)).astype(jnp.bfloat16)
    result = features + lax.dot_general(
        gated_rows, out_weight, (((1,), (1,)), ((), ())), preferred_element_type=jnp.float32
    )
    saved_state = (
        normed_in,
        preact,
        gate_part,
        value_portion,
        query_portion,
        key_portion,
        score_list,
        weight_pieces,
        normed,
        inverse,
        gated_rows,
    )
    return (result, saved_state)


def layer_backward(upstream, saved_state, attend_mask, out_weight, batch_count):
    (
        normed_in,
        preact,
        gate_part,
        value_portion,
        query_portion,
        key_portion,
        score_list,
        weight_pieces,
        normed,
        inverse,
        gated_rows,
    ) = saved_state
    hidden_width = out_weight.shape[1]
    scoring_scale = HEAD_DIM ** (-0.5)
    upstream_b = upstream.astype(jnp.bfloat16)
    grad_gated = jnp.dot(upstream_b, out_weight, preferred_element_type=jnp.float32)
    grad_gate = grad_gated * normed
    grad_normed = grad_gated * gate_part.astype(jnp.float32)
    grad_attended = inverse * (
        grad_normed
        - jnp.mean(grad_normed, -1, keepdims=True)
        - normed * jnp.mean(grad_normed * normed, -1, keepdims=True)
    )
    grad_attended = grad_attended.astype(jnp.bfloat16).reshape(batch_count, -1, hidden_width)
    value_gradient, query_gradient, key_gradient = ([], [], [])
    for current_head in range(HEADS):
        column_begin = current_head * HEAD_DIM
        column_end = column_begin + HEAD_DIM
        gradient_portion = grad_attended[..., column_begin:column_end]
        weight_gradient = batch_stacked(
            "ptx,pux->ptu", gradient_portion, value_portion[..., column_begin:column_end]
        )
        value_gradient.append(
            batch_stacked("hyo,hyx->hox", weight_pieces[current_head], gradient_portion)
        )
        score_gradient = (
            weight_gradient * attend_mask * silu_slope(score_list[current_head]) * scoring_scale
        ).astype(jnp.bfloat16)
        query_gradient.append(
            batch_stacked("fjz,fzy->fjy", score_gradient, key_portion[..., column_begin:column_end])
        )
        key_gradient.append(
            batch_stacked(
                "hyo,hyx->hox", score_gradient, query_portion[..., column_begin:column_end]
            )
        )
    grad_project = jnp.concatenate(
        [
            grad_gate,
            jnp.concatenate(value_gradient, -1).reshape(-1, hidden_width),
            jnp.concatenate(query_gradient, -1).reshape(-1, hidden_width),
            jnp.concatenate(key_gradient, -1).reshape(-1, hidden_width),
        ],
        -1,
    )
    grad_preact = (grad_project * silu_slope(preact)).astype(jnp.bfloat16)
    return (normed_in, grad_preact, upstream_b, gated_rows)


def item_scores(result, cand_rows):
    length_out = jnp.sqrt(jnp.sum(result * result, -1, keepdims=True) + epsilon)
    single_output = result / length_out
    row_float = cand_rows.astype(jnp.float32)
    row_length = jnp.sqrt(jnp.sum(row_float * row_float, -1, keepdims=True) + epsilon)
    single_row = row_float / row_length
    logit_values = jnp.sum(single_output[:, None, :] * single_row, -1) / softmax_warmth
    exponent = jnp.exp(logit_values)
    softmax_weights = exponent / jnp.sum(exponent, -1, keepdims=True)
    logit_gradient = softmax_weights - (jnp.arange(NCAND) == 0).astype(jnp.float32)[None, :]
    gathered_rows = jnp.sum(logit_gradient[..., None] * single_row, 1) / softmax_warmth
    upstream = (
        gathered_rows - single_output * jnp.sum(single_output * gathered_rows, -1, keepdims=True)
    ) / length_out
    scattered_rows = logit_gradient[..., None] * single_output[:, None, :] / softmax_warmth
    grad_rows = (
        (scattered_rows - single_row * jnp.sum(single_row * scattered_rows, -1, keepdims=True))
        / row_length
    ).astype(jnp.bfloat16)
    return (upstream, grad_rows)


def body(events, lengths, destinations, history, negatives, in_weight, out_weight, item_table):
    owners = lax.axis_size("seq")
    hidden_width = out_weight.shape[1]
    tok_rows = events.shape[0]
    slot_rows = 3 * tok_rows // (2 * owners)
    user_lengths = lengths[0]
    user_dests = destinations[0]
    starts = jnp.cumsum(user_lengths) - user_lengths
    candidates = jnp.concatenate([history[:, None], negatives], 1)
    chosen_user = (user_dests[None, :] == jnp.arange(owners)[:, None]).astype(jnp.int32)
    send_length = jnp.sum(chosen_user * user_lengths[None, :], 1)
    send_start = jnp.sum(chosen_user * starts[None, :], 1)
    slot_index = jnp.arange(slot_rows)
    filled = slot_index[None, :] < send_length[:, None]
    sources = jnp.clip(send_start[:, None] + slot_index[None, :], 0, tok_rows - 1)
    send_tokens = jnp.where(filled[..., None], events[sources], jnp.zeros((), jnp.bfloat16))
    send_items = jnp.where(filled[..., None], candidates[sources], 0)
    got_tokens, got_items, got_length = (
        lax.all_to_all(send_tokens, "seq", split_axis=0, concat_axis=0, tiled=True),
        lax.all_to_all(send_items, "seq", split_axis=0, concat_axis=0, tiled=True),
        lax.all_to_all(send_length[:, None], "seq", split_axis=0, concat_axis=0, tiled=True),
    )
    counts = got_length[:, 0]
    block_ends = jnp.cumsum(counts)
    offsets = block_ends - counts
    positions = jnp.arange(tok_rows)
    anchor = jnp.minimum(
        jnp.sum((block_ends[None, :] <= positions[:, None]).astype(jnp.int32), 1), owners - 1
    )
    placed = anchor * slot_rows + positions - offsets[anchor]
    slot_tokens = got_tokens.reshape(owners * slot_rows, D)
    relayed_items = got_items.reshape(owners * slot_rows, NCAND)[placed]
    attend_mask = (
        (anchor[:, None] == anchor[None, :]) & (positions[None, :] <= positions[:, None])
    ).astype(jnp.float32)[None]
    batch_count = 1
    result_rows, saved_state = layer_forward(
        slot_tokens[placed], attend_mask, in_weight, out_weight, batch_count
    )
    per_owner = tok_rows * NCAND // owners
    flat_items = relayed_items.reshape(-1)
    owner_order = jnp.argsort(flat_items // VOCAB_DEV, stable=True)
    asked_rows = (flat_items % VOCAB_DEV)[owner_order].reshape(owners, per_owner)
    requested = lax.all_to_all(asked_rows, "seq", split_axis=0, concat_axis=0, tiled=True)
    found_rows = item_table[requested]
    fetched, requested = (
        lax.all_to_all(found_rows, "seq", split_axis=0, concat_axis=0, tiled=True),
        requested,
    )
    cand_rows = (
        jnp.zeros((tok_rows * NCAND, D), jnp.bfloat16)
        .at[owner_order]
        .set(fetched.reshape(-1, D))
        .reshape(tok_rows, NCAND, D)
    )
    upstream, grad_rows = item_scores(result_rows, cand_rows)
    outgoing = grad_rows.reshape(-1, D)[owner_order].reshape(owners, per_owner, D)
    returned = lax.all_to_all(outgoing, "seq", split_axis=0, concat_axis=0, tiled=True)
    table_part = jax.ops.segment_sum(
        returned.reshape(-1, D).astype(jnp.float32), requested.reshape(-1), num_segments=VOCAB_DEV
    )
    normed_in, grad_preact, upstream_b, gated_rows = layer_backward(
        upstream, saved_state, attend_mask, out_weight, batch_count
    )
    first_term = lax.dot_general(
        lax.slice_in_dim(normed_in, 0, lax.axis_size("seq") * (D // owners), axis=1),
        grad_preact,
        (((0,), (0,)), ((), ())),
        preferred_element_type=jnp.float32,
    )
    second_term = lax.dot_general(
        lax.slice_in_dim(upstream_b, 0, lax.axis_size("seq") * (D // owners), axis=1),
        gated_rows,
        (((0,), (0,)), ((), ())),
        preferred_element_type=jnp.float32,
    )
    weight_shard = lax.psum_scatter(
        jnp.concatenate([first_term, second_term], 1).astype(jnp.bfloat16),
        "seq",
        scatter_dimension=0,
        tiled=True,
    ).astype(jnp.float32)
    table_grad, weight_shard = (
        lax.psum(table_part.astype(jnp.bfloat16), "grp").astype(jnp.float32),
        lax.psum(weight_shard.astype(jnp.bfloat16), "grp").astype(jnp.float32),
    )
    layer_out = result_rows.astype(jnp.bfloat16)
    return (
        layer_out,
        weight_shard[:, : 4 * hidden_width],
        weight_shard[:, 4 * hidden_width :],
        table_grad,
    )


def solution(mesh):
    return jax.shard_map(
        body,
        mesh=mesh,
        in_specs=(
            P(("grp", "seq"), None),
            P(("grp", "seq"), None),
            P(("grp", "seq"), None),
            P(("grp", "seq")),
            P(("grp", "seq"), None),
            P(),
            P(),
            P("seq", None),
        ),
        out_specs=(P(("grp", "seq"), None), P("seq", None), P("seq", None), P("seq", None)),
        check_vma=False,
    )
```

profile of v0, /device:TPU:32, one launch (start us, length us, event | category | flops | bytes accessed | tf_op | source)
XLA Modules:
  0.0 399.3 jit_solution(15326774801198506185)
XLA Ops:
  7.2 1.0 reduce-window_clone.1
  10.3 8.6 %all-to-all-start.1 = ((s32[16,1,1]{2,1,0:T(1,128)}), s32[16,1,1]{2,1,0:T(1,128)S(1)}, u32[]{:S(2)}, u32[]{:S(2)}) async-start(s32[16,1,1]{2,1,0:T(1,128)} %copy.95), calls=%async_computation.1 | async-start | bytes 16384 | tf_op jit(solution)/shard_map/all_to_all | solution.py:191
  20.0 1.1 gather_fusion.2
  21.9 2.1 gather_fusion
  24.0 1.0 all-to-all-done.1
  25.0 6.2 %all-to-all-start.2 = ((s32[16,24,4]{1,2,0:T(4,128)}), s32[16,24,4]{1,2,0:T(4,128)S(1)}, u32[]{:S(2)}, u32[]{:S(2)}) async-start(s32[16,24,4]{1,2,0:T(4,128)} %broadcast_select_fusion.1), calls=%async_computation.2 | async-start | bytes 65536 | tf_op jit(solution)/shard_map/all_to_all | solution.py:190
  32.6 4.3 %compare_select_fusion.5 = (s32[256,1]{0,1:T(1,128)S(1)}, s32[256,1]{0,1:T(1,128)S(1)}) fusion(s32[]{:T(128)} %bitcast.17, s32[]{:T(128)} %bitcast.18, s32[]{:T(128)} %bitcast.19, s32[]{:T(128)} %bitcast.20, s32[]{:T(128)} %bitcast.21, s32[]{:T(128)} %bitcast.23, s32[]{:T(128)} %bitcast.22, s32[256,1]{0,1:T(1,128)S(1)} %bitcast.229), kind=kLoop, calls=%fused_computation.155 | loop fusion | flops 3840 | bytes 3100 | tf_op jit(solution)/shard_map/gather | solution.py:200
  37.0 5.7 %select_select_fusion = s32[256]{0:T(256)S(1)} fusion(pred[256]{0:T(512)(128)(4,1)S(1)} %get-tuple-element.16, pred[256]{0:T(512)(128)(4,1)S(1)} %get-tuple-element.15, pred[256]{0:T(512)(128)(4,1)S(1)} %get-tuple-element.14, pred[256]{0:T(512)(128)(4,1)S(1)} %get-tuple-element.13, pred[256]{0:T(512)(128)(4,1)S(1)} %get-tuple-element.12, ...), kind=kLoop, calls=%fused_computation.165 | loop fusion | flops 2304 | bytes 4388 | tf_op jit(solution)/shard_map/gather | solution.py:200
  43.8 4.4 %sort.17 = (s32[1024]{0:T(1024)}, s32[1024]{0:T(1024)S(1)}) sort(s32[1024]{0:T(1024)S(1)} %get-tuple-element.33, s32[1024]{0:T(1024)S(1)} %iota.37), dimensions={0}, to_apply=%region_13.14 | sort | flops 10240 | bytes 16384 | tf_op jit(solution)/shard_map/jit(argsort)/sort | solution.py:212
  48.2 4.5 %gather_fusion.4 = s32[1024]{0:T(1024)S(1)} fusion(s32[1024]{0:T(1024)S(1)} %get-tuple-element.32, s32[1024]{0:T(1024)S(1)} %get-tuple-element.30), kind=kCustom, calls=%fused_computation.4 | custom fusion | bytes 12288 | tf_op jit(solution)/shard_map/gather | solution.py:213
  53.4 7.2 %all-to-all-start.3 = ((s32[16,1,64]{2,1,0:T(1,128)}), s32[16,1,64]{2,1,0:T(1,128)S(1)}, u32[]{:S(2)}, u32[]{:S(2)}) async-start(s32[16,1,64]{2,1,0:T(1,128)} %all_to_all.30), calls=%async_computation.3 | async-start | bytes 16384 | tf_op jit(solution)/shard_map/all_to_all | solution.py:214
  60.6 1.0 broadcast_select_fusion
  61.6 5.1 %all-to-all-done.3 = s32[16,1,64]{2,1,0:T(1,128)S(1)} async-done(((s32[16,1,64]{2,1,0:T(1,128)}), s32[16,1,64]{2,1,0:T(1,128)S(1)}, u32[]{:S(2)}, u32[]{:S(2)}) %all-to-all-start.3) | async-done | bytes 4128 | tf_op jit(solution)/shard_map/all_to_all | solution.py:214
  66.8 4.9 %all-to-all-start = ((bf16[16,24,1024]{2,1,0:T(8,128)(2,1)}), bf16[16,24,1024]{2,1,0:T(8,128)(2,1)S(1)}, u32[]{:S(2)}, u32[]{:S(2)}) async-start(bf16[16,24,1024]{2,1,0:T(8,128)(2,1)} %broadcast_select_fusion), calls=%async_computation | async-start | bytes 1572864 | tf_op jit(solution)/shard_map/all_to_all | solution.py:189
  72.2 5.4 %gather_fusion.5 = bf16[1024,1024]{1,0:T(8,128)(2,1)} fusion(bf16[512,1024]{1,0:T(8,128)(2,1)S(1)} %copy-done, s32[1024]{0:T(1024)S(1)} %broadcast_clamp_fusion), kind=kCustom, calls=%fused_computation.5 | custom fusion | bytes 4198400 | tf_op jit(solution)/shard_map/gather | solution.py:215
  77.6 13.0 %all-to-all-done = bf16[16,24,1024]{2,1,0:T(8,128)(2,1)S(1)} async-done(((bf16[16,24,1024]{2,1,0:T(8,128)(2,1)}), bf16[16,24,1024]{2,1,0:T(8,128)(2,1)S(1)}, u32[]{:S(2)}, u32[]{:S(2)}) %all-to-all-start) | async-done | bytes 786464 | tf_op jit(solution)/shard_map/all_to_all | solution.py:189
  90.6 6.9 %all-to-all-start.4 = ((bf16[16,64,1024]{2,1,0:T(8,128)(2,1)}), bf16[16,64,1024]{2,1,0:T(8,128)(2,1)}, u32[]{:S(2)}, u32[]{:S(2)}) async-start(bf16[16,64,1024]{2,1,0:T(8,128)(2,1)} %bitcast.201), calls=%async_computation.4 | async-start | bytes 4194304 | tf_op jit(solution)/shard_map/all_to_all | solution.py:217
  97.7 1.2 gather_fusion.1
  99.4 4.9 %multiply_convert_fusion = (bf16[256,2048]{1,0:T(8,128)(2,1)S(1)}, f32[256,2048]{1,0:T(8,128)}) fusion(bf16[1024,2048]{1,0:T(8,128)(2,1)} %param.13, bf16[256,1024]{1,0:T(8,128)(2,1)S(1)} %gather_fusion.1, f32[256]{0:T(256)S(1)} %add_rsqrt_fusion.1, f32[256]{0:T(256)S(1)} %broadcast_multiply_fusion.2), kind=kOutput, calls=%fused_computation.22 | convolution fusion | flops 1077411840 | bytes 7866368 | tf_op jit(solution)/shard_map/dot_general | solution.py:36
  105.0 1.0 select_convert_fusion.2
  107.6 1.8 multiply_reduce_fusion.5
  109.6 0.9 broadcast_divide_fusion.1
  110.4 3.1 mul.315
  113.6 5.4 %mul.316 = f32[1024,1024]{1,0:T(8,128)} reshape(f32[256,4,1024]{2,1,0:T(4,128)} %mul.315) | data formatting | bytes 8388608 | tf_op jit(solution)/shard_map/mul | solution.py:155
  118.9 25.8 %all-to-all-done.4 = bf16[16,64,1024]{2,1,0:T(8,128)(2,1)} async-done(((bf16[16,64,1024]{2,1,0:T(8,128)(2,1)}), bf16[16,64,1024]{2,1,0:T(8,128)(2,1)}, u32[]{:S(2)}, u32[]{:S(2)}) %all-to-all-start.4) | async-done | bytes 2097184 | tf_op jit(solution)/shard_map/all_to_all | solution.py:217
  144.7 6.8 %scatter_custom_fusion = bf16[1024,1024]{1,0:T(8,128)(2,1)S(1)} fusion(s32[1024]{0:T(1024)S(1)} %get-tuple-element.31, bf16[1024,1024]{1,0:T(8,128)(2,1)} %bitcast.52, bf16[]{:T(256)} %constant.83.clone.1), kind=kCustom, calls=%fused_computation.67 | custom fusion | bytes 2097664 | tf_op jit(solution)/shard_map/scatter | solution.py:223
  152.0 3.0 reshape.577
  155.0 0.8 sqrt.22
  155.8 2.9 multiply_reduce_fusion.2
  159.3 1.5 exp.43
  160.8 1.5 reduce_sum.190
  162.3 1.0 divide_subtract_fusion
  163.4 4.6 %multiply_reduce_fusion.1 = f32[256,1024]{1,0:T(8,128)S(1)} fusion(f32[256,4,1024]{2,1,0:T(4,128)} %reshape.577, f32[256,4]{1,0:T(8,128)} %sqrt.22, f32[256,4]{1,0:T(8,128)S(1)} %divide_subtract_fusion), kind=kLoop, calls=%fused_computation.15 | loop fusion | flops 2883584 | bytes 5251072 | tf_op jit(solution)/shard_map/reduce_sum | solution.py:159
  175.8 0.9 copy-done.6
  177.4 1.6 convolution_convert_fusion
  179.0 2.7 pad_maximum_fusion
  182.8 3.3 multiply_reduce_fusion
  186.2 2.6 divide_convert_fusion
  188.8 5.3 %gather_fusion.6 = bf16[1024,1024]{1,0:T(8,128)(2,1)} fusion(bf16[1024,1024]{1,0:T(8,128)(2,1)S(1)} %divide_convert_fusion, s32[1024]{0:T(1024)S(1)} %copy-done.34), kind=kCustom, calls=%fused_computation.6 | custom fusion | bytes 4198400 | tf_op jit(solution)/shard_map/gather | solution.py:227
  194.1 6.8 %all-to-all-start.5 = ((bf16[16,64,1024]{2,1,0:T(8,128)(2,1)}), bf16[16,64,1024]{2,1,0:T(8,128)(2,1)S(1)}, u32[]{:S(2)}, u32[]{:S(2)}) async-start(bf16[16,64,1024]{2,1,0:T(8,128)(2,1)} %bitcast.202), calls=%async_computation.6 | async-start | bytes 4194304 | tf_op jit(solution)/shard_map/all_to_all | solution.py:228
  202.5 55.5 %all-to-all-done.5 = bf16[16,64,1024]{2,1,0:T(8,128)(2,1)S(1)} async-done(((bf16[16,64,1024]{2,1,0:T(8,128)(2,1)}), bf16[16,64,1024]{2,1,0:T(8,128)(2,1)S(1)}, u32[]{:S(2)}, u32[]{:S(2)}) %all-to-all-start.5) | async-done | bytes 2097184 | tf_op jit(solution)/shard_map/all_to_all | solution.py:228
  258.0 10.4 %scatter_custom_fusion.1 = f32[512,1024]{1,0:T(8,128)} fusion(s32[1024]{0:T(1024)S(1)} %reshape.668, bf16[1024,1024]{1,0:T(8,128)(2,1)S(1)} %bitcast.203, f32[]{:T(128)} %constant.88.clone.1), kind=kCustom, calls=%fused_computation.10 | custom fusion | flops 2097152 | bytes 4194308 | tf_op jit(solution)/shard_map/scatter-add | solution.py:229
  268.4 2.8 convert_element_type.134
  271.2 11.9 %reduce-scatter.2.cloned.1.call-done = bf16[64,2560]{1,0:T(8,128)(2,1)} async-done(((bf16[1024,2560]{1,0:T(8,128)(2,1)}), bf16[64,2560]{1,0:T(8,128)(2,1)}) %reduce-scatter.2.cloned.1.call-update) | async-done | bytes 327696 | tf_op jit(solution)/shard_map/reduce_scatter | solution.py:247
  283.1 103.2 %all-reduce.3.cloned.1.call-done = (bf16[64,2560]{1,0:T(8,128)(2,1)}, bf16[512,1024]{1,0:T(8,128)(2,1)}) async-done(((bf16[64,2560]{1,0:T(8,128)(2,1)}, bf16[512,1024]{1,0:T(8,128)(2,1)}), (bf16[64,2560]{1,0:T(8,128)(2,1)}, bf16[512,1024]{1,0:T(8,128)(2,1)})) %all-reduce.3.cloned.1.call-update) | async-done | bytes 1376272 | tf_op jit(solution)/shard_map/psum | solution.py:255
  386.3 1.9 slice.151
  388.2 1.5 slice.152
  389.7 2.8 convert_element_type.135
  (196 shorter events, 22.6 us)
Async XLA Ops:
  7.2 65.1 %copy-start = (bf16[512,1024]{1,0:T(8,128)(2,1)S(1)}, bf16[512,1024]{1,0:T(8,128)(2,1)}, u32[]{:S(2)}) copy-start(bf16[512,1024]{1,0:T(8,128)(2,1)} %param.15) | copy-start | bytes 3145732
  7.2 14.7 %copy-start.3 = (bf16[256,1024]{1,0:T(8,128)(2,1)S(1)}, bf16[256,1024]{1,0:T(8,128)(2,1)}, u32[]{:S(2)}) copy-start(bf16[256,1024]{1,0:T(8,128)(2,1)} %param.8) | copy-start | bytes 1572868
  10.3 14.7 %all-to-all-start.1 = ((s32[16,1,1]{2,1,0:T(1,128)}), s32[16,1,1]{2,1,0:T(1,128)S(1)}, u32[]{:S(2)}, u32[]{:S(2)}) async-start(s32[16,1,1]{2,1,0:T(1,128)} %copy.95), calls=%async_computation.1 | async-start | bytes 16384 | tf_op jit(solution)/shard_map/all_to_all | solution.py:191
  25.0 17.7 %all-to-all-start.2 = ((s32[16,24,4]{1,2,0:T(4,128)}), s32[16,24,4]{1,2,0:T(4,128)S(1)}, u32[]{:S(2)}, u32[]{:S(2)}) async-start(s32[16,24,4]{1,2,0:T(4,128)} %broadcast_select_fusion.1), calls=%async_computation.2 | async-start | bytes 65536 | tf_op jit(solution)/shard_map/all_to_all | solution.py:190
  32.6 72.4 %copy-start.40 = (s32[256]{0:T(256)}, s32[256]{0:T(256)S(1)}, u32[]{:S(2)}) copy-start(s32[256]{0:T(256)S(1)} %broadcast_minimum_fusion) | copy-start | bytes 3076
  48.2 4.5 %copy-start.33 = (s32[1024]{0:T(1024)}, s32[1024]{0:T(1024)S(1)}, u32[]{:S(2)}) copy-start(s32[1024]{0:T(1024)S(1)} %get-tuple-element.30) | copy-start | bytes 12292
  53.4 13.4 %all-to-all-start.3 = ((s32[16,1,64]{2,1,0:T(1,128)}), s32[16,1,64]{2,1,0:T(1,128)S(1)}, u32[]{:S(2)}, u32[]{:S(2)}) async-start(s32[16,1,64]{2,1,0:T(1,128)} %all_to_all.30), calls=%async_computation.3 | async-start | bytes 16384 | tf_op jit(solution)/shard_map/all_to_all | solution.py:214
  66.8 23.8 %all-to-all-start = ((bf16[16,24,1024]{2,1,0:T(8,128)(2,1)}), bf16[16,24,1024]{2,1,0:T(8,128)(2,1)S(1)}, u32[]{:S(2)}, u32[]{:S(2)}) async-start(bf16[16,24,1024]{2,1,0:T(8,128)(2,1)} %broadcast_select_fusion), calls=%async_computation | async-start | bytes 1572864 | tf_op jit(solution)/shard_map/all_to_all | solution.py:189
  90.6 54.1 %all-to-all-start.4 = ((bf16[16,64,1024]{2,1,0:T(8,128)(2,1)}), bf16[16,64,1024]{2,1,0:T(8,128)(2,1)}, u32[]{:S(2)}, u32[]{:S(2)}) async-start(bf16[16,64,1024]{2,1,0:T(8,128)(2,1)} %bitcast.201), calls=%async_computation.4 | async-start | bytes 4194304 | tf_op jit(solution)/shard_map/all_to_all | solution.py:217
  97.5 185.5 %reduce-scatter.2.cloned.1.call-start = ((), (), s32[]{:S(2)}) async-start(), calls=%async_computation.7 | async-start | bytes 5570560 | tf_op jit(solution)/shard_map/reduce_scatter | solution.py:247
  98.9 8.7 %copy-start.5 = (bf16[256,1024]{1,0:T(8,128)(2,1)}, bf16[256,1024]{1,0:T(8,128)(2,1)S(1)}, u32[]{:S(2)}) copy-start(bf16[256,1024]{1,0:T(8,128)(2,1)S(1)} %gather_fusion.1) | copy-start | bytes 1572868
  99.1 5.2 %copy-start.42 = (f32[256]{0:T(256)}, f32[256]{0:T(256)S(1)}, u32[]{:S(2)}) copy-start(f32[256]{0:T(256)S(1)} %broadcast_multiply_fusion.2) | copy-start | bytes 3076
  99.4 4.9 %copy-start.47 = (f32[256]{0:T(256)}, f32[256]{0:T(256)S(1)}, u32[]{:S(2)}) copy-start(f32[256]{0:T(256)S(1)} %add_rsqrt_fusion.1) | copy-start | bytes 3076
  104.3 3.3 copy-start.17
  104.3 1.6 copy-start.7
  104.4 2.7 copy-start.15
  104.6 1.4 copy-start.29
  104.8 1.2 copy-start.27
  106.0 3.5 copy-start.19
  106.0 3.5 copy-start.21
  106.0 3.5 copy-start.23
  106.0 3.5 copy-start.25
  106.7 2.8 copy-start.9
  107.0 2.5 copy-start.11
  107.4 2.1 copy-start.13
  107.4 2.1 copy-start.36
  107.6 1.9 copy-start.44
  109.5 4.0 %copy-start.38 = (f32[256]{0:T(256)}, f32[256]{0:T(256)S(1)}, u32[]{:S(2)}) copy-start(f32[256]{0:T(256)S(1)} %add_sqrt_fusion.1) | copy-start | bytes 3076
  151.5 31.2 %copy-start.2 = (bf16[1024,1024]{1,0:T(8,128)(2,1)}, bf16[1024,1024]{1,0:T(8,128)(2,1)S(1)}, u32[]{:S(2)}) copy-start(bf16[1024,1024]{1,0:T(8,128)(2,1)S(1)} %scatter_custom_fusion) | copy-start | bytes 6291460
  168.0 1.4 copy-start.18
  168.0 1.4 copy-start.37
  168.0 1.4 copy-start.45
  168.1 1.7 copy-start.49
  170.3 1.2 copy-start.22
  170.4 1.4 copy-start.20
  170.4 1.6 copy-start.16
  170.4 1.6 copy-start.30
  170.4 1.6 copy-start.41
  170.7 1.6 copy-start.32
  172.3 1.4 copy-start.50
  175.7 1.0 copy-start.6
  175.7 1.0 copy-start.43
  175.7 1.8 copy-start.51
  182.8 3.5 copy-start.4
  186.2 2.6 copy-start.34
  194.1 63.8 %all-to-all-start.5 = ((bf16[16,64,1024]{2,1,0:T(8,128)(2,1)}), bf16[16,64,1024]{2,1,0:T(8,128)(2,1)S(1)}, u32[]{:S(2)}, u32[]{:S(2)}) async-start(bf16[16,64,1024]{2,1,0:T(8,128)(2,1)} %bitcast.202), calls=%async_computation.6 | async-start | bytes 4194304 | tf_op jit(solution)/shard_map/all_to_all | solution.py:228
  200.9 185.4 %all-reduce.3.cloned.1.call-start = ((), (), s32[]{:S(2)}) async-start(), calls=%async_computation.8 | async-start | bytes 2752512 | tf_op jit(solution)/shard_map/psum | solution.py:255
  386.3 6.2 %copy-start.1 = (bf16[512,1024]{1,0:T(8,128)(2,1)S(1)}, bf16[512,1024]{1,0:T(8,128)(2,1)}, u32[]{:S(2)}) copy-start(bf16[512,1024]{1,0:T(8,128)(2,1)} %param.15) | copy-start | bytes 3145732
  (12 other events, 10.6 us)
Sparse Core Ops, SparseCore 0:
  181.9 101.0 reduce-scatter.1
  286.4 99.8 all-reduce.2
where the time goes:
time: 401 us; the launch traced here: 399 us
  waiting for transfers between devices  216 us (54%)
  other arithmetic  59.3 us (15%)
  local copies, waits for them, and re-layouts  53.1 us (13%)
  starting transfers between devices  41.1 us (10%)
  matrix products  15.2 us (4%)
  between operations  15.1 us (4%)
    psum x1, waiting for transfers between devices, body(): lax.psum(weight_shard.astype(jnp.bfloat16), 'grp').astype(jnp.float32)  103 us
    all_to_all x1, waiting for transfers between devices, body(): lax.all_to_all(outgoing, 'seq', split_axis=0, concat_axis=0, tiled=True)  55.5 us
    all_to_all x1, waiting for transfers between devices, body(): lax.all_to_all(found_rows, 'seq', split_axis=0, concat_axis=0, tiled=True)  25.8 us
    all_to_all x1, waiting for transfers between devices, body(): lax.all_to_all(send_tokens, 'seq', split_axis=0, concat_axis=0, tiled=True)  13 us
    reduce_scatter x1, waiting for transfers between devices, body(): lax.psum_scatter(jnp.concatenate([first_term, second_term], 1).astype(jnp...  11.9 us
    scatter-add x1, other arithmetic, body(): jax.ops.segment_sum(returned.reshape(-1, D).astype(jnp.float32), requeste...  10.4 us
    gather x3, other arithmetic, body(): placed = anchor * slot_rows + positions - offsets[anchor]  10.1 us
    all_to_all x1, starting transfers between devices, body(): lax.all_to_all(send_length[:, None], 'seq', split_axis=0, concat_axis=0,...  8.59 us
  transfers between devices with their start and end apart: 8, of which 7 were waited for; matrix products, arithmetic and copies ran while one was open for 18% of the time, Pallas kernels for 0%

commit v1 on v0

--- a/solution.py
+++ b/solution.py
@@ -10,6 +10,11 @@
 VOCAB_DEV = 512
 epsilon = 1e-05
 softmax_warmth = 0.05
+
+
+def add_all(block, axis):
+    parts = lax.all_gather(block, axis)
+    return jnp.sum(parts, axis=0)
 
 
 def center_scale(values):
@@ -252,7 +257,7 @@
     ).astype(jnp.float32)
     table_grad, weight_shard = (
         lax.psum(table_part.astype(jnp.bfloat16), "grp").astype(jnp.float32),
-        lax.psum(weight_shard.astype(jnp.bfloat16), "grp").astype(jnp.float32),
+        add_all(weight_shard.astype(jnp.bfloat16), "grp").astype(jnp.float32),
     )
     layer_out = result_rows.astype(jnp.bfloat16)
     return (

time: 401 us -> 448 us (1.12)
  waiting for transfers between devices: 216 us -> 259 us
    all_gather x0 -> x1, waiting for transfers between devices: none -> 59.9 us  [add_all(): parts = lax.all_gather(block, axis)]
    psum x1, waiting for transfers between devices: 103 us -> 86.9 us  [body(): lax.psum(table_part.astype(jnp.bfloat16), 'grp').astype(jnp.float32)]
  transfers between devices with their start and end apart: 8 -> 9, of which waited for: 7 -> 8; matrix products, arithmetic and copies ran while one was open for 18% -> 16% of each run, Pallas kernels for 0% -> 0%
where the time goes in v1:
time: 448 us; the launch traced here: 446 us
  waiting for transfers between devices  259 us (58%)
  other arithmetic  62.6 us (14%)
  local copies, waits for them, and re-layouts  51.2 us (11%)
  starting transfers between devices  41.2 us (9%)
  between operations  16.5 us (4%)
  matrix products  15.2 us (3%)
    psum x1, waiting for transfers between devices, body(): lax.psum(table_part.astype(jnp.bfloat16), 'grp').astype(jnp.float32)  86.9 us
    all_gather x1, waiting for transfers between devices, add_all(): parts = lax.all_gather(block, axis)  59.9 us
    all_to_all x1, waiting for transfers between devices, body(): lax.all_to_all(outgoing, 'seq', split_axis=0, concat_axis=0, tiled=True)  55.5 us
    all_to_all x1, waiting for transfers between devices, body(): lax.all_to_all(found_rows, 'seq', split_axis=0, concat_axis=0, tiled=True)  25.8 us
    all_to_all x1, waiting for transfers between devices, body(): lax.all_to_all(send_tokens, 'seq', split_axis=0, concat_axis=0, tiled=True)  13 us
    reduce_scatter x1, waiting for transfers between devices, body(): lax.psum_scatter(jnp.concatenate([first_term, second_term], 1).astype(jnp...  11.8 us
    scatter-add x1, other arithmetic, body(): jax.ops.segment_sum(returned.reshape(-1, D).astype(jnp.float32), requeste...  10.4 us
    gather x3, other arithmetic, body(): placed = anchor * slot_rows + positions - offsets[anchor]  10.1 us
  transfers between devices with their start and end apart: 9, of which 8 were waited for; matrix products, arithmetic and copies ran while one was open for 16% of the time, Pallas kernels for 0%

profile of v1, /device:TPU:32, one launch (start us, length us, event | category | flops | bytes accessed | tf_op | source)
XLA Modules:
  0.0 445.8 jit_solution(17509701312399798320)
XLA Ops:
  8.0 1.0 reduce-window_clone.1
  11.1 8.6 %all-to-all-start.1 = ((s32[16,1,1]{2,1,0:T(1,128)}), s32[16,1,1]{2,1,0:T(1,128)S(1)}, u32[]{:S(2)}, u32[]{:S(2)}) async-start(s32[16,1,1]{2,1,0:T(1,128)} %copy.95), calls=%async_computation.1 | async-start | bytes 16384 | tf_op jit(solution)/shard_map/all_to_all | solution.py:196
  20.8 1.1 gather_fusion.2
  22.7 2.1 gather_fusion
  24.8 1.0 all-to-all-done.1
  25.8 6.2 %all-to-all-start.2 = ((s32[16,24,4]{1,2,0:T(4,128)}), s32[16,24,4]{1,2,0:T(4,128)S(1)}, u32[]{:S(2)}, u32[]{:S(2)}) async-start(s32[16,24,4]{1,2,0:T(4,128)} %broadcast_select_fusion.1), calls=%async_computation.2 | async-start | bytes 65536 | tf_op jit(solution)/shard_map/all_to_all | solution.py:195
  33.4 4.3 compare_select_fusion.5
  37.8 5.7 %select_select_fusion = s32[256]{0:T(256)S(1)} fusion(pred[256]{0:T(512)(128)(4,1)S(1)} %get-tuple-element.16, pred[256]{0:T(512)(128)(4,1)S(1)} %get-tuple-element.15, pred[256]{0:T(512)(128)(4,1)S(1)} %get-tuple-element.14, pred[256]{0:T(512)(128)(4,1)S(1)} %get-tuple-element.13, pred[256]{0:T(512)(128)(4,1)S(1)} %get-tuple-element.12, ...), kind=kLoop, calls=%fused_computation.165 | loop fusion | flops 2304 | bytes 4388 | tf_op jit(solution)/shard_map/gather | solution.py:205
  44.6 4.4 sort.17
  49.0 4.5 %gather_fusion.4 = s32[1024]{0:T(1024)S(1)} fusion(s32[1024]{0:T(1024)S(1)} %get-tuple-element.30, s32[1024]{0:T(1024)S(1)} %get-tuple-element.28), kind=kCustom, calls=%fused_computation.4 | custom fusion | bytes 12288 | tf_op jit(solution)/shard_map/gather | solution.py:218
  54.2 7.2 %all-to-all-start.3 = ((s32[16,1,64]{2,1,0:T(1,128)}), s32[16,1,64]{2,1,0:T(1,128)S(1)}, u32[]{:S(2)}, u32[]{:S(2)}) async-start(s32[16,1,64]{2,1,0:T(1,128)} %all_to_all.30), calls=%async_computation.3 | async-start | bytes 16384 | tf_op jit(solution)/shard_map/all_to_all | solution.py:219
  61.4 1.0 broadcast_select_fusion
  62.4 5.1 %all-to-all-done.3 = s32[16,1,64]{2,1,0:T(1,128)S(1)} async-done(((s32[16,1,64]{2,1,0:T(1,128)}), s32[16,1,64]{2,1,0:T(1,128)S(1)}, u32[]{:S(2)}, u32[]{:S(2)}) %all-to-all-start.3) | async-done | bytes 4128 | tf_op jit(solution)/shard_map/all_to_all | solution.py:219
  67.6 4.9 %all-to-all-start = ((bf16[16,24,1024]{2,1,0:T(8,128)(2,1)}), bf16[16,24,1024]{2,1,0:T(8,128)(2,1)S(1)}, u32[]{:S(2)}, u32[]{:S(2)}) async-start(bf16[16,24,1024]{2,1,0:T(8,128)(2,1)} %broadcast_select_fusion), calls=%async_computation | async-start | bytes 1572864 | tf_op jit(solution)/shard_map/all_to_all | solution.py:194
  73.1 5.4 %gather_fusion.5 = bf16[1024,1024]{1,0:T(8,128)(2,1)} fusion(bf16[512,1024]{1,0:T(8,128)(2,1)S(1)} %copy-done, s32[1024]{0:T(1024)S(1)} %broadcast_clamp_fusion), kind=kCustom, calls=%fused_computation.5 | custom fusion | bytes 4198400 | tf_op jit(solution)/shard_map/gather | solution.py:220
  78.4 13.0 %all-to-all-done = bf16[16,24,1024]{2,1,0:T(8,128)(2,1)S(1)} async-done(((bf16[16,24,1024]{2,1,0:T(8,128)(2,1)}), bf16[16,24,1024]{2,1,0:T(8,128)(2,1)S(1)}, u32[]{:S(2)}, u32[]{:S(2)}) %all-to-all-start) | async-done | bytes 786464 | tf_op jit(solution)/shard_map/all_to_all | solution.py:194
  91.4 6.9 %all-to-all-start.4 = ((bf16[16,64,1024]{2,1,0:T(8,128)(2,1)}), bf16[16,64,1024]{2,1,0:T(8,128)(2,1)}, u32[]{:S(2)}, u32[]{:S(2)}) async-start(bf16[16,64,1024]{2,1,0:T(8,128)(2,1)} %bitcast.202), calls=%async_computation.4 | async-start | bytes 4194304 | tf_op jit(solution)/shard_map/all_to_all | solution.py:222
  98.6 1.2 gather_fusion.1
  100.2 4.9 %multiply_convert_fusion = (bf16[256,2048]{1,0:T(8,128)(2,1)S(1)}, f32[256,2048]{1,0:T(8,128)}) fusion(bf16[1024,2048]{1,0:T(8,128)(2,1)} %param.13, bf16[256,1024]{1,0:T(8,128)(2,1)S(1)} %gather_fusion.1, f32[256]{0:T(256)S(1)} %add_rsqrt_fusion.1, f32[256]{0:T(256)S(1)} %broadcast_multiply_fusion.2), kind=kOutput, calls=%fused_computation.22 | convolution fusion | flops 1077411840 | bytes 7866368 | tf_op jit(solution)/shard_map/dot_general | solution.py:41
  105.8 1.0 select_convert_fusion.2
  108.5 1.8 multiply_reduce_fusion.5
  110.4 0.9 broadcast_divide_fusion.1
  111.3 3.1 mul.315
  114.4 5.4 %mul.316 = f32[1024,1024]{1,0:T(8,128)} reshape(f32[256,4,1024]{2,1,0:T(4,128)} %mul.315) | data formatting | bytes 8388608 | tf_op jit(solution)/shard_map/mul | solution.py:160
  119.8 25.8 %all-to-all-done.4 = bf16[16,64,1024]{2,1,0:T(8,128)(2,1)} async-done(((bf16[16,64,1024]{2,1,0:T(8,128)(2,1)}), bf16[16,64,1024]{2,1,0:T(8,128)(2,1)}, u32[]{:S(2)}, u32[]{:S(2)}) %all-to-all-start.4) | async-done | bytes 2097184 | tf_op jit(solution)/shard_map/all_to_all | solution.py:222
  145.5 6.8 %scatter_custom_fusion = bf16[1024,1024]{1,0:T(8,128)(2,1)S(1)} fusion(s32[1024]{0:T(1024)S(1)} %get-tuple-element.29, bf16[1024,1024]{1,0:T(8,128)(2,1)} %bitcast.52, bf16[]{:T(256)} %constant.84.clone.1), kind=kCustom, calls=%fused_computation.67 | custom fusion | bytes 2097664 | tf_op jit(solution)/shard_map/scatter | solution.py:228
  152.8 3.0 reshape.577
  156.7 2.9 multiply_reduce_fusion.2
  160.2 1.5 exp.43
  161.6 1.5 reduce_sum.202
  163.2 1.0 divide_subtract_fusion
  164.2 4.6 %multiply_reduce_fusion.1 = f32[256,1024]{1,0:T(8,128)S(1)} fusion(f32[256,4,1024]{2,1,0:T(4,128)} %reshape.577, f32[256,4]{1,0:T(8,128)} %sqrt.22, f32[256,4]{1,0:T(8,128)S(1)} %divide_subtract_fusion), kind=kLoop, calls=%fused_computation.15 | loop fusion | flops 2883584 | bytes 5251072 | tf_op jit(solution)/shard_map/reduce_sum | solution.py:164
  176.7 0.9 copy-done.6
  178.3 1.6 convolution_convert_fusion
  179.9 2.7 pad_maximum_fusion
  183.6 3.3 multiply_reduce_fusion
  187.0 2.6 divide_convert_fusion
  189.6 5.3 %gather_fusion.6 = bf16[1024,1024]{1,0:T(8,128)(2,1)} fusion(bf16[1024,1024]{1,0:T(8,128)(2,1)S(1)} %divide_convert_fusion, s32[1024]{0:T(1024)S(1)} %copy-done.34), kind=kCustom, calls=%fused_computation.6 | custom fusion | bytes 4198400 | tf_op jit(solution)/shard_map/gather | solution.py:232
  195.0 6.8 %all-to-all-start.5 = ((bf16[16,64,1024]{2,1,0:T(8,128)(2,1)}), bf16[16,64,1024]{2,1,0:T(8,128)(2,1)S(1)}, u32[]{:S(2)}, u32[]{:S(2)}) async-start(bf16[16,64,1024]{2,1,0:T(8,128)(2,1)} %bitcast.203), calls=%async_computation.6 | async-start | bytes 4194304 | tf_op jit(solution)/shard_map/all_to_all | solution.py:233
  203.3 55.5 %all-to-all-done.5 = bf16[16,64,1024]{2,1,0:T(8,128)(2,1)S(1)} async-done(((bf16[16,64,1024]{2,1,0:T(8,128)(2,1)}), bf16[16,64,1024]{2,1,0:T(8,128)(2,1)S(1)}, u32[]{:S(2)}, u32[]{:S(2)}) %all-to-all-start.5) | async-done | bytes 2097184 | tf_op jit(solution)/shard_map/all_to_all | solution.py:233
  258.8 10.4 %scatter_custom_fusion.1 = f32[512,1024]{1,0:T(8,128)} fusion(s32[1024]{0:T(1024)S(1)} %reshape.668, bf16[1024,1024]{1,0:T(8,128)(2,1)S(1)} %bitcast.204, f32[]{:T(128)} %constant.89.clone.1), kind=kCustom, calls=%fused_computation.10 | custom fusion | flops 2097152 | bytes 4194308 | tf_op jit(solution)/shard_map/scatter-add | solution.py:234
  269.2 2.8 convert_element_type.136
  272.1 11.8 %reduce-scatter.2.cloned.1.call-done = bf16[64,2560]{1,0:T(8,128)(2,1)} async-done(((bf16[1024,2560]{1,0:T(8,128)(2,1)}), bf16[64,2560]{1,0:T(8,128)(2,1)}) %reduce-scatter.2.cloned.1.call-update) | async-done | bytes 327696 | tf_op jit(solution)/shard_map/reduce_scatter | solution.py:252
  283.9 86.9 %all-reduce.2.cloned.1.call-done = bf16[512,1024]{1,0:T(8,128)(2,1)} async-done(((bf16[512,1024]{1,0:T(8,128)(2,1)}), bf16[512,1024]{1,0:T(8,128)(2,1)}) %all-reduce.2.cloned.1.call-update) | async-done | bytes 1048592 | tf_op jit(solution)/shard_map/psum | solution.py:259
  370.8 2.8 convert_element_type.137
  373.6 59.9 %all-gather.3.cloned.1.call-done = bf16[1024,2560]{1,0:T(8,128)(2,1)} async-done(((bf16[64,2560]{1,0:T(8,128)(2,1)}), bf16[1024,2560]{1,0:T(8,128)(2,1)}) %all-gather.3.cloned.1.call-update) | async-done | bytes 5242896 | tf_op jit(solution)/shard_map/all_gather | solution.py:16
  433.5 3.3 reduce_sum.207
  436.8 0.8 slice.151
  (200 shorter events, 24.1 us)
Async XLA Ops:
  8.0 65.1 %copy-start = (bf16[512,1024]{1,0:T(8,128)(2,1)S(1)}, bf16[512,1024]{1,0:T(8,128)(2,1)}, u32[]{:S(2)}) copy-start(bf16[512,1024]{1,0:T(8,128)(2,1)} %param.15) | copy-start | bytes 3145732
  8.0 14.7 %copy-start.3 = (bf16[256,1024]{1,0:T(8,128)(2,1)S(1)}, bf16[256,1024]{1,0:T(8,128)(2,1)}, u32[]{:S(2)}) copy-start(bf16[256,1024]{1,0:T(8,128)(2,1)} %param.8) | copy-start | bytes 1572868
  11.1 14.7 %all-to-all-start.1 = ((s32[16,1,1]{2,1,0:T(1,128)}), s32[16,1,1]{2,1,0:T(1,128)S(1)}, u32[]{:S(2)}, u32[]{:S(2)}) async-start(s32[16,1,1]{2,1,0:T(1,128)} %copy.95), calls=%async_computation.1 | async-start | bytes 16384 | tf_op jit(solution)/shard_map/all_to_all | solution.py:196
  25.8 17.7 %all-to-all-start.2 = ((s32[16,24,4]{1,2,0:T(4,128)}), s32[16,24,4]{1,2,0:T(4,128)S(1)}, u32[]{:S(2)}, u32[]{:S(2)}) async-start(s32[16,24,4]{1,2,0:T(4,128)} %broadcast_select_fusion.1), calls=%async_computation.2 | async-start | bytes 65536 | tf_op jit(solution)/shard_map/all_to_all | solution.py:195
  33.4 72.4 %copy-start.40 = (s32[256]{0:T(256)}, s32[256]{0:T(256)S(1)}, u32[]{:S(2)}) copy-start(s32[256]{0:T(256)S(1)} %broadcast_minimum_fusion) | copy-start | bytes 3076
  49.0 4.5 %copy-start.33 = (s32[1024]{0:T(1024)}, s32[1024]{0:T(1024)S(1)}, u32[]{:S(2)}) copy-start(s32[1024]{0:T(1024)S(1)} %get-tuple-element.28) | copy-start | bytes 12292
  54.2 13.4 %all-to-all-start.3 = ((s32[16,1,64]{2,1,0:T(1,128)}), s32[16,1,64]{2,1,0:T(1,128)S(1)}, u32[]{:S(2)}, u32[]{:S(2)}) async-start(s32[16,1,64]{2,1,0:T(1,128)} %all_to_all.30), calls=%async_computation.3 | async-start | bytes 16384 | tf_op jit(solution)/shard_map/all_to_all | solution.py:219
  67.6 23.8 %all-to-all-start = ((bf16[16,24,1024]{2,1,0:T(8,128)(2,1)}), bf16[16,24,1024]{2,1,0:T(8,128)(2,1)S(1)}, u32[]{:S(2)}, u32[]{:S(2)}) async-start(bf16[16,24,1024]{2,1,0:T(8,128)(2,1)} %broadcast_select_fusion), calls=%async_computation | async-start | bytes 1572864 | tf_op jit(solution)/shard_map/all_to_all | solution.py:194
  91.4 54.1 %all-to-all-start.4 = ((bf16[16,64,1024]{2,1,0:T(8,128)(2,1)}), bf16[16,64,1024]{2,1,0:T(8,128)(2,1)}, u32[]{:S(2)}, u32[]{:S(2)}) async-start(bf16[16,64,1024]{2,1,0:T(8,128)(2,1)} %bitcast.202), calls=%async_computation.4 | async-start | bytes 4194304 | tf_op jit(solution)/shard_map/all_to_all | solution.py:222
  98.3 185.5 %reduce-scatter.2.cloned.1.call-start = ((), (), s32[]{:S(2)}) async-start(), calls=%async_computation.7 | async-start | bytes 5570560 | tf_op jit(solution)/shard_map/reduce_scatter | solution.py:252
  99.7 8.7 %copy-start.5 = (bf16[256,1024]{1,0:T(8,128)(2,1)}, bf16[256,1024]{1,0:T(8,128)(2,1)S(1)}, u32[]{:S(2)}) copy-start(bf16[256,1024]{1,0:T(8,128)(2,1)S(1)} %gather_fusion.1) | copy-start | bytes 1572868
  99.9 5.2 %copy-start.42 = (f32[256]{0:T(256)}, f32[256]{0:T(256)S(1)}, u32[]{:S(2)}) copy-start(f32[256]{0:T(256)S(1)} %broadcast_multiply_fusion.2) | copy-start | bytes 3076
  100.2 4.9 %copy-start.47 = (f32[256]{0:T(256)}, f32[256]{0:T(256)S(1)}, u32[]{:S(2)}) copy-start(f32[256]{0:T(256)S(1)} %add_rsqrt_fusion.1) | copy-start | bytes 3076
  105.1 3.3 copy-start.17
  105.2 1.6 copy-start.7
  105.2 2.7 copy-start.15
  105.4 1.4 copy-start.29
  105.6 1.2 copy-start.27
  106.8 3.5 copy-start.19
  106.8 3.5 copy-start.21
  106.8 3.5 copy-start.23
  106.8 3.5 copy-start.25
  107.5 2.8 copy-start.9
  107.8 2.5 copy-start.11
  108.2 2.1 copy-start.13
  108.2 2.1 copy-start.36
  108.5 1.9 copy-start.44
  110.4 4.0 copy-start.38
  152.3 31.2 %copy-start.2 = (bf16[1024,1024]{1,0:T(8,128)(2,1)}, bf16[1024,1024]{1,0:T(8,128)(2,1)S(1)}, u32[]{:S(2)}) copy-start(bf16[1024,1024]{1,0:T(8,128)(2,1)S(1)} %scatter_custom_fusion) | copy-start | bytes 6291460
  168.9 1.4 copy-start.18
  168.9 1.4 copy-start.37
  168.9 1.4 copy-start.45
  168.9 1.7 copy-start.49
  171.2 1.2 copy-start.22
  171.2 1.4 copy-start.20
  171.2 1.6 copy-start.16
  171.2 1.6 copy-start.30
  171.2 1.6 copy-start.41
  171.5 1.6 copy-start.32
  173.1 1.4 copy-start.50
  176.5 1.0 copy-start.6
  176.5 1.8 copy-start.51
  183.6 3.5 copy-start.4
  187.0 2.6 copy-start.34
  195.0 63.8 %all-to-all-start.5 = ((bf16[16,64,1024]{2,1,0:T(8,128)(2,1)}), bf16[16,64,1024]{2,1,0:T(8,128)(2,1)S(1)}, u32[]{:S(2)}, u32[]{:S(2)}) async-start(bf16[16,64,1024]{2,1,0:T(8,128)(2,1)} %bitcast.203), calls=%async_computation.6 | async-start | bytes 4194304 | tf_op jit(solution)/shard_map/all_to_all | solution.py:233
  201.7 169.1 %all-reduce.2.cloned.1.call-start = ((), (), s32[]{:S(2)}) async-start(), calls=%async_computation.8 | async-start | bytes 2097152 | tf_op jit(solution)/shard_map/psum | solution.py:259
  272.0 161.5 %all-gather.3.cloned.1.call-start = ((), (), s32[]{:S(2)}) async-start(), calls=%async_computation.9 | async-start | bytes 5570560 | tf_op jit(solution)/shard_map/all_gather | solution.py:16
  433.5 4.8 %copy-start.1 = (bf16[512,1024]{1,0:T(8,128)(2,1)S(1)}, bf16[512,1024]{1,0:T(8,128)(2,1)}, u32[]{:S(2)}) copy-start(bf16[512,1024]{1,0:T(8,128)(2,1)} %param.15) | copy-start | bytes 3145732
  (13 other events, 11.6 us)
Sparse Core Ops, SparseCore 0:
  182.7 101.0 reduce-scatter.1
Sparse Core Ops, SparseCore 1:
  272.1 98.7 all-reduce.1
  373.2 60.3 all-gather.2
